TPU v7x, 32 devices: a whole 2x2x4 slice. The times are simulated.
32 devices in a mesh: wide: 4 (over z), step: 2 (over x), img: 4 (over y, core).
Axes of the slice: x: 2, y: 2, z: 4, core: 2. Of those that a mesh axis runs over, the one named last changes fastest.
Arguments:
- activations: bfloat16 [2, 8, 4096, 2560], P('step', 'img', 'wide'), may hold values from -6 to 6
- cotangents: bfloat16 [2, 8, 4096, 10240], P('step', 'img', 'wide'), may hold values from -6 to 6
- projection: bfloat16 [2560, 512], P('wide'), may hold values from -0.125 to 0.125
- buckets: int32 [10240], replicated, may hold values from 0 to 63
- sign_bits: int32 [10240], replicated, may hold values from 0 to 1
- timesteps: int32 [2, 8], P('step', 'img'), may hold values from 0 to 999
Outputs:
- sketch: float32 [8, 32768], P('img', ('wide', 'step'))
Inputs may be any that keep to these rules, and one draw needn't show every extreme that they name: `buckets`: every hidden unit has one bucket.
All inputs are finite; a program needn't handle non-finite values.
Results may differ from a plain program's by a relative error of at most 0.003.
Values may be sent and summed in bfloat16 or wider, within the bound.
No kernel may reach another device: no remote copies, remote signals or barrier semaphores. Data moves between devices by JAX's collectives and lax.ppermute only.
A program may use at most 320 MiB of HBM per device.

v0:
```python
import jax
import jax.numpy as jnp
from jax import lax
from jax.sharding import PartitionSpec as P

RW = 512
KB = 64
DIFF_STEPS = 1000


def local(activations, cotangents, projection, buckets, sign_bits, timesteps):
    image_count = activations.shape[1]
    projected = jnp.einsum(
        "sipd,dr->sipr",
        activations,
        lax.all_gather(projection, "wide", axis=0, tiled=True),
        preferred_element_type=jnp.float32,
    ).astype(jnp.bfloat16)
    weight = 2.0 - 1.5 * timesteps.astype(jnp.float32) / DIFF_STEPS
    sign_vals = (2 * sign_bits - 1).astype(jnp.float32)
    bucket_ids = jnp.arange(KB, dtype=jnp.int32)
    columns = lax.all_to_all(cotangents, "wide", split_axis=3, concat_axis=2, tiled=True)
    col_count = columns.shape[3]
    col_grads = jnp.einsum(
        "sipc,sipr->sicr",
        columns,
        lax.all_gather(projected, "wide", axis=2, tiled=True),
        preferred_element_type=jnp.float32,
    )
    unit = col_grads * lax.rsqrt(jnp.sum(col_grads * col_grads, axis=3, keepdims=True) + 1e-06)
    col_start = lax.axis_index("wide") * col_count
    local_buckets = lax.dynamic_slice_in_dim(buckets, col_start, col_count, 0)
    local_signs = lax.dynamic_slice_in_dim(sign_vals, col_start, col_count, 0)
    bucket_table = jnp.where(
        local_buckets[:, None] == bucket_ids[None, :], local_signs[:, None], 0.0
    )
    sketch_part = jnp.einsum("ck,sicr->sikr", bucket_table, unit, precision=lax.Precision.HIGHEST)
    scaled = sketch_part * weight[:, :, None, None]
    partial_terms = jnp.sum(scaled, axis=0).reshape(image_count, KB * RW)
    return lax.psum_scatter(partial_terms, ("wide", "step"), scatter_dimension=1, tiled=True)


def solution(mesh):
    in_specs = (
        P("step", "img", "wide", None),
        P("step", "img", "wide", None),
        P("wide", None),
        P(),
        P(),
        P("step", "img"),
    )
    out_specs = P("img", ("wide", "step"))
    return jax.shard_map(local, mesh=mesh, in_specs=in_specs, out_specs=out_specs, check_vma=False)
```

profile of v0, /device:TPU:0, one launch (start us, length us, event | category | flops | bytes accessed | tf_op | source)
XLA Modules:
  0.0 1637.5 jit_solution(14158558723203348897)
XLA Ops:
  6.5 102.0 %copy.9 = bf16[1,2,1024,10240]{2,1,0,3:T(2,128)(2,1)} copy(bf16[1,2,1024,10240]{3,2,1,0:T(8,128)(2,1)} %param.7) | data formatting | bytes 83886080 | tf_op args[1]
  108.5 11.2 all-to-all-start
  119.7 0.0 all-gather.4.cloned.1.call-start
  119.7 0.7 all-gather.4.cloned.1.call-update
  120.4 0.0 copy-start
  120.4 0.0 all-gather.6.cloned.1.call-start
  120.5 293.3 %all-gather.4.cloned.1.call-done = bf16[2560,512]{1,0:T(8,128)(2,1)} async-done(((bf16[640,512]{1,0:T(8,128)(2,1)}), bf16[2560,512]{1,0:T(8,128)(2,1)}) %all-gather.4.cloned.1.call-update) | async-done | bytes 2621456 | tf_op jit(solution)/shard_map/all_gather | solution.py:16
  413.8 10.2 fusion.7
  424.0 0.0 all-gather.6.cloned.1.call-update
  424.0 0.0 reduce-scatter.4.cloned.1.call-start
  424.1 0.8 dynamic_slice.6
  424.9 0.8 fusion.27
  425.7 0.0 copy-done
  425.7 774.8 %all-to-all-done = bf16[1,2,1024,10240]{2,1,0,3:T(2,128)(2,1)} async-done(((bf16[1,2,1024,10240]{2,1,0,3:T(2,128)(2,1)}), bf16[1,2,1024,10240]{2,1,0,3:T(2,128)(2,1)}, u32[]{:S(2)}, u32[]{:S(2)}) %all-to-all-start) | async-done | bytes 41943072 | tf_op jit(solution)/shard_map/all_to_all | solution.py:22
  1200.5 101.1 %copy.10 = bf16[1,2,1024,4,2560]{4,2,3,1,0:T(8,128)(2,1)} copy(bf16[1,2,1024,4,2560]{2,1,4,3,0:T(2,128)(2,1)} %bitcast.2) | data formatting | bytes 83886080 | tf_op jit(solution)/shard_map/all_to_all | solution.py:22
  1301.6 0.0 all-gather.6.cloned.1.call-done
  1301.6 27.9 %multiply_reduce_fusion = (f32[2,2560]{1,0:T(2,128)S(1)}, f32[2,512,2560]{2,1,0:T(8,128)S(1)}) fusion(bf16[2,4096,512]{1,2,0:T(8,128)(2,1)} %all-gather.6.cloned.1.call-done, bf16[2,4096,2560]{2,1,0:T(8,128)(2,1)} %bitcast.43), kind=kOutput, calls=%fused_computation.5 | convolution fusion | flops 21480075264 | bytes 60837888 | tf_op jit(solution)/shard_map/sipc,sipr->sicr/dot_general | solution.py:24
  1329.5 10.6 fusion.18
  1340.1 8.6 copy.15
  1348.6 0.0 reduce-scatter.4.cloned.1.call-update
  1348.7 279.5 %reduce-scatter.4.cloned.1.call-done = f32[4096,2]{1,0:T(8,128)} async-done(((f32[32768,2]{1,0:T(8,128)}), f32[4096,2]{1,0:T(8,128)}) %reduce-scatter.4.cloned.1.call-update) | async-done | bytes 32784
  1628.2 2.8 copy.14
  (2 shorter events, 0.0 us)
Async XLA Ops:
  108.5 1092.0 %all-to-all-start = ((bf16[1,2,1024,10240]{2,1,0,3:T(2,128)(2,1)}), bf16[1,2,1024,10240]{2,1,0,3:T(2,128)(2,1)}, u32[]{:S(2)}, u32[]{:S(2)}) async-start(bf16[1,2,1024,10240]{2,1,0,3:T(2,128)(2,1)} %copy.9), calls=%async_computation | async-start | bytes 83886080 | tf_op jit(solution)/shard_map/all_to_all | solution.py:22
  119.7 294.1 %all-gather.4.cloned.1.call-start = ((), (), s32[]{:S(2)}) async-start(), calls=%async_computation.2 | async-start | bytes 3276800 | tf_op jit(solution)/shard_map/all_gather | solution.py:16
  120.4 305.3 %copy-start = (s32[1,2]{1,0:T(1,128)S(1)}, s32[1,2]{1,0:T(1,128)}, u32[]{:S(2)}) copy-start(s32[1,2]{1,0:T(1,128)} %param.11) | copy-start | bytes 28
  120.4 1181.1 %all-gather.6.cloned.1.call-start = ((), (), s32[]{:S(2)}) async-start(), calls=%async_computation.3 | async-start | bytes 10485760 | tf_op jit(solution)/shard_map/all_gather | solution.py:27
  424.0 1204.1 %reduce-scatter.4.cloned.1.call-start = ((), (), s32[]{:S(2)}) async-start(), calls=%async_computation.4 | async-start | bytes 18874368
Sparse Core Ops, SparseCore 0:
  122.1 291.7 all-gather.3
  424.2 278.0 all-gather.5
  1348.8 279.3 reduce-scatter.3
where the time goes:
time: 1640 us
  waiting for transfers between devices  1350 us (82%)
  local copies, waits for them, and re-layouts  215 us (13%)
  matrix products  48.7 us (3%)
    all_to_all x1, waiting for transfers between devices, local(): lax.all_to_all(cotangents, 'wide', split_axis=3, concat_axis=2, tiled=True)  775 us
    all_gather x1, waiting for transfers between devices, local(): lax.all_gather(projection, 'wide', axis=0, tiled=True)  293 us
    unnamed x4, waiting for transfers between devices  280 us
    unnamed x5, local copies, waits for them, and re-layouts  113 us
    all_to_all x1, local copies, waits for them, and re-layouts, local(): lax.all_to_all(cotangents, 'wide', split_axis=3, concat_axis=2, tiled=True)  101 us
  transfers between devices with their start and end apart: 4, of which 3 were waited for; matrix products, arithmetic and copies ran while one was open for 7% of the time, Pallas kernels for 0%

commit v1 on v0

--- a/solution.py
+++ b/solution.py
@@ -1,3 +1,4 @@
+import functools
 import jax
 import jax.numpy as jnp
 from jax import lax
@@ -6,6 +7,18 @@
 RW = 512
 KB = 64
 DIFF_STEPS = 1000
+
+
+def load_waves(inp, at_axis, on_dim):
+    mid_arr = lax.axis_size("wide")
+    heard = jnp.split(inp, mid_arr, at_axis)
+    new = jnp.stack(heard)
+    opened = lax.all_to_all(new, axis_name="wide", split_axis=0, concat_axis=0)
+    low = jnp.concatenate(opened, on_dim)
+    return low
+
+
+perform_slabs = functools.partial(load_waves, at_axis=3, on_dim=2)
 
 
 def local(activations, cotangents, projection, buckets, sign_bits, timesteps):
@@ -19,7 +32,7 @@
     weight = 2.0 - 1.5 * timesteps.astype(jnp.float32) / DIFF_STEPS
     sign_vals = (2 * sign_bits - 1).astype(jnp.float32)
     bucket_ids = jnp.arange(KB, dtype=jnp.int32)
-    columns = lax.all_to_all(cotangents, "wide", split_axis=3, concat_axis=2, tiled=True)
+    columns = perform_slabs(cotangents)
     col_count = columns.shape[3]
     col_grads = jnp.einsum(
         "sipc,sipr->sicr",

time: 1640 us -> 1520 us (0.927)
  local copies, waits for them, and re-layouts: 215 us -> 69.3 us
  other arithmetic: 0.82 us -> 29.4 us
    unnamed x5 -> x4, local copies, waits for them, and re-layouts: 113 us -> 11.4 us
    all_to_all x1 -> x0, local copies, waits for them, and re-layouts: 101 us -> none  [local(): lax.all_to_all(cotangents, 'wide', split_axis=3, concat_axis=2, tiled=True)]
    another operation x0 -> x1, local copies, waits for them, and re-layouts: none -> 28.7 us  [load_waves(): new = jnp.stack(heard)]
    another operation x0 -> x1, other arithmetic: none -> 28.6 us  [load_waves(): new = jnp.stack(heard)]
    reshape x0 -> x1, local copies, waits for them, and re-layouts: none -> 28.4 us  [load_waves(): low = jnp.concatenate(opened, on_dim)]
  transfers between devices with their start and end apart: 4 -> 4, of which waited for: 3 -> 3; matrix products, arithmetic and copies ran while one was open for 7% -> 3% of each run, Pallas kernels for 0% -> 0%
where the time goes in v1:
time: 1520 us
  waiting for transfers between devices  1350 us (89%)
  local copies, waits for them, and re-layouts  69.3 us (5%)
  matrix products  48.7 us (3%)
  other arithmetic  29.4 us (2%)
    all_to_all x1, waiting for transfers between devices, load_waves(): opened = lax.all_to_all(new, axis_name='wide', split_axis=0, concat_axis=0)  775 us
    all_gather x1, waiting for transfers between devices, local(): lax.all_gather(projection, 'wide', axis=0, tiled=True)  293 us
    unnamed x4, waiting for transfers between devices  280 us
  transfers between devices with their start and end apart: 4, of which 3 were waited for; matrix products, arithmetic and copies ran while one was open for 3% of the time, Pallas kernels for 0%

profile of v1, /device:TPU:0, one launch (start us, length us, event | category | flops | bytes accessed | tf_op | source)
XLA Modules:
  0.0 1520.1 jit_solution(10425926994783141363)
XLA Ops:
  6.5 28.7 %slice_bitcast_fusion.3 = (bf16[1,1,2,1024,2560]{4,3,2,1,0:T(8,128)(2,1)}, bf16[1,1,2,1024,2560]{4,3,2,1,0:T(8,128)(2,1)}, bf16[1,1,2,1024,2560]{4,3,2,1,0:T(8,128)(2,1)}, bf16[1,1,2,1024,2560]{4,3,2,1,0:T(8,128)(2,1)}) fusion(bf16[1,2,1024,10240]{3,2,1,0:T(8,128)(2,1)} %param.7), kind=kLoop, calls=%fused_computation.9 | loop fusion | bytes 83886080 | tf_op jit(solution)/shard_map/stack | solution.py:15
  35.2 28.6 %pad_maximum_fusion = bf16[4,1,2,1024,2560]{4,3,2,1,0:T(8,128)(2,1)} fusion(bf16[1,1,2,1024,2560]{4,3,2,1,0:T(8,128)(2,1)} %get-tuple-element.7, bf16[1,1,2,1024,2560]{4,3,2,1,0:T(8,128)(2,1)} %get-tuple-element.8, bf16[1,1,2,1024,2560]{4,3,2,1,0:T(8,128)(2,1)} %get-tuple-element.6, bf16[1,1,2,1024,2560]{4,3,2,1,0:T(8,128)(2,1)} %get-tuple-element.5), kind=kLoop, calls=%fused_computation | loop fusion | flops 62914560 | bytes 83886080 | tf_op jit(solution)/shard_map/stack | solution.py:15
  63.8 11.2 all-to-all-start
  75.0 0.0 all-gather.4.cloned.1.call-start
  75.0 0.7 all-gather.4.cloned.1.call-update
  75.7 0.0 copy-start
  75.7 0.0 all-gather.6.cloned.1.call-start
  75.8 293.5 %all-gather.4.cloned.1.call-done = bf16[2560,512]{1,0:T(8,128)(2,1)} async-done(((bf16[640,512]{1,0:T(8,128)(2,1)}), bf16[2560,512]{1,0:T(8,128)(2,1)}) %all-gather.4.cloned.1.call-update) | async-done | bytes 2621456 | tf_op jit(solution)/shard_map/all_gather | solution.py:29
  369.3 10.2 fusion.6
  379.4 0.0 all-gather.6.cloned.1.call-update
  379.5 0.0 reduce-scatter.4.cloned.1.call-start
  379.5 0.8 dynamic_slice.6
  380.3 0.8 fusion.26
  381.1 0.0 copy-done
  381.1 774.7 %all-to-all-done = bf16[4,1,2,1024,2560]{4,3,2,1,0:T(8,128)(2,1)} async-done(((bf16[4,1,2,1024,2560]{4,3,2,1,0:T(8,128)(2,1)}), bf16[4,1,2,1024,2560]{4,3,2,1,0:T(8,128)(2,1)}, u32[]{:S(2)}, u32[]{:S(2)}) %all-to-all-start) | async-done | bytes 41943072 | tf_op jit(solution)/shard_map/all_to_all | solution.py:16
  1155.8 28.4 %copy.9 = bf16[1,2,4,1024,2560]{4,3,2,1,0:T(8,128)(2,1)} copy(bf16[1,2,4,1024,2560]{4,3,1,0,2:T(8,128)(2,1)} %bitcast.4) | data formatting | bytes 83886080 | tf_op jit(solution)/shard_map/reshape | solution.py:17
  1184.3 0.0 all-gather.6.cloned.1.call-done
  1184.3 27.9 %multiply_reduce_fusion = (f32[2,2560]{1,0:T(2,128)S(1)}, f32[2,2560,512]{1,2,0:T(8,128)S(1)}) fusion(bf16[2,4096,512]{1,2,0:T(8,128)(2,1)} %all-gather.6.cloned.1.call-done, bf16[2,4096,2560]{2,1,0:T(8,128)(2,1)} %bitcast.40), kind=kOutput, calls=%fused_computation.5 | convolution fusion | flops 21480075264 | bytes 60837888 | tf_op jit(solution)/shard_map/sipc,sipr->sicr/dot_general | solution.py:37
  1212.2 10.6 fusion.17
  1222.8 8.6 copy.14
  1231.3 0.0 reduce-scatter.4.cloned.1.call-update
  1231.4 279.4 %reduce-scatter.4.cloned.1.call-done = f32[4096,2]{1,0:T(8,128)} async-done(((f32[32768,2]{1,0:T(8,128)}), f32[4096,2]{1,0:T(8,128)}) %reduce-scatter.4.cloned.1.call-update) | async-done | bytes 32784
  1510.8 2.8 copy.13
  (2 shorter events, 0.0 us)
Async XLA Ops:
  63.8 1092.0 %all-to-all-start = ((bf16[4,1,2,1024,2560]{4,3,2,1,0:T(8,128)(2,1)}), bf16[4,1,2,1024,2560]{4,3,2,1,0:T(8,128)(2,1)}, u32[]{:S(2)}, u32[]{:S(2)}) async-start(bf16[4,1,2,1024,2560]{4,3,2,1,0:T(8,128)(2,1)} %pad_maximum_fusion), calls=%async_computation | async-start | bytes 83886080 | tf_op jit(solution)/shard_map/all_to_all | solution.py:16
  75.0 294.3 %all-gather.4.cloned.1.call-start = ((), (), s32[]{:S(2)}) async-start(), calls=%async_computation.2 | async-start | bytes 3276800 | tf_op jit(solution)/shard_map/all_gather | solution.py:29
  75.7 305.4 %copy-start = (s32[1,2]{1,0:T(1,128)S(1)}, s32[1,2]{1,0:T(1,128)}, u32[]{:S(2)}) copy-start(s32[1,2]{1,0:T(1,128)} %param.11) | copy-start | bytes 28
  75.7 1108.5 %all-gather.6.cloned.1.call-start = ((), (), s32[]{:S(2)}) async-start(), calls=%async_computation.3 | async-start | bytes 10485760 | tf_op jit(solution)/shard_map/all_gather | solution.py:40
  379.5 1131.3 %reduce-scatter.4.cloned.1.call-start = ((), (), s32[]{:S(2)}) async-start(), calls=%async_computation.4 | async-start | bytes 18874368
Sparse Core Ops, SparseCore 0:
  77.4 291.8 all-gather.3
  379.6 277.9 all-gather.5
  1231.5 279.2 reduce-scatter.3
